TPU v7x, 512 devices: a whole 4x8x8 slice. The times are simulated.
512 devices in a mesh: expert: 64 (over y, x, core), hidden: 8 (over z).
Axes of the slice: x: 4, y: 8, z: 8, core: 2. Of those that a mesh axis runs over, the one named last changes fastest.
Arguments:
- tokens: bfloat16 [4096, 4096], P('expert', 'hidden'), may hold values from -6 to 6
- expert_ids: int32 [4096, 8], P('expert'), may hold values from 0 to 63, all different within a row; in each aligned block of 64 rows (0 to 63, 64 to 127, ...) at most 16 rows name the same one
- gate_weights: float32 [4096, 8], P('expert'), may hold values from 0.05 to 0.5
- gate_proj: bfloat16 [64, 1536, 4096], P('expert', 'hidden'), may hold values from -0.09375 to 0.09375
- up_proj: bfloat16 [64, 1536, 4096], P('expert', 'hidden'), may hold values from -0.09375 to 0.09375
- down_proj: bfloat16 [64, 1536, 4096], P('expert', None, 'hidden'), may hold values from -0.15625 to 0.15625
Outputs:
- moe_out: bfloat16 [4096, 4096], P('expert', 'hidden')
Inputs may be any that keep to these rules, and one draw needn't show every extreme that they name: `expert_ids`: each row names 8 different experts; in each aligned block of 64 rows no expert is named by more than 16 rows.
All inputs are finite; a program needn't handle non-finite values.
Results may differ from a plain program's by a relative error of at most 0.0057.
Values may be sent and summed in bfloat16 or wider, within the bound.
No kernel may reach another device: no remote copies, remote signals or barrier semaphores. Data moves between devices by JAX's collectives and lax.ppermute only.
A program may use at most 64 MiB of HBM per device.

v0:
```python
import jax
import jax.numpy as jnp
from jax import lax
from jax.sharding import PartitionSpec as P


def on_device(tokens, expert_ids, gate_weights, gate_proj, up_proj, down_proj):
    local_count = gate_proj.shape[0]
    experts_all = local_count * lax.axis_size("expert")
    tok_rows = tokens.shape[0]
    top_count = expert_ids.shape[1]
    capacity = 2 * tok_rows * top_count // experts_all
    flat_ids = expert_ids.reshape(-1)
    onehot = (flat_ids[:, None] == jnp.arange(experts_all, dtype=jnp.int32)[None, :]).astype(
        jnp.int32
    )
    slot_index = jnp.sum((jnp.cumsum(onehot, axis=0) - onehot) * onehot, axis=1)
    position = flat_ids * capacity + slot_index
    token_of = jnp.arange(tok_rows * top_count, dtype=jnp.int32) // top_count
    full_rows = lax.all_gather(tokens, "hidden", axis=1, tiled=True)
    packed = jnp.zeros((experts_all * capacity, full_rows.shape[1]), full_rows.dtype)
    packed = packed.at[position].set(full_rows[token_of])
    arrived = lax.all_to_all(
        packed.reshape(experts_all, capacity, full_rows.shape[1]),
        "expert",
        split_axis=0,
        concat_axis=1,
        tiled=True,
    )
    gate_sum = jnp.einsum("lrd,lfd->lfr", arrived, gate_proj, preferred_element_type=jnp.float32)
    up_sum = jnp.einsum("lrd,lfd->lfr", arrived, up_proj, preferred_element_type=jnp.float32)
    activation = (jax.nn.silu(gate_sum) * up_sum).astype(jnp.bfloat16)
    expert_out = jnp.einsum(
        "lfr,lfd->lrd",
        lax.all_gather(activation, "hidden", axis=1, tiled=True),
        down_proj,
        preferred_element_type=jnp.float32,
    ).astype(jnp.bfloat16)
    returned = lax.all_to_all(expert_out, "expert", split_axis=1, concat_axis=0, tiled=True)
    gathered = returned.reshape(experts_all * capacity, returned.shape[2])[position]
    gathered = gathered.reshape(tok_rows, top_count, returned.shape[2]).astype(jnp.float32)
    mixed = jnp.sum(gathered * gate_weights[:, :, None], axis=1)
    return mixed.astype(jnp.bfloat16)


def solution(mesh):
    in_specs = (
        P("expert", "hidden"),
        P("expert", None),
        P("expert", None),
        P("expert", "hidden", None),
        P("expert", "hidden", None),
        P("expert", None, "hidden"),
    )
    out_specs = P("expert", "hidden")
    return jax.shard_map(
        on_device, mesh=mesh, in_specs=in_specs, out_specs=out_specs, check_vma=False
    )
```

profile of v0, /device:TPU:1, one launch (start us, length us, event | category | flops | bytes accessed | tf_op | source)
XLA Modules:
  0.0 375.7 jit_solution(17025929349063810798)
XLA Ops:
  6.5 0.0 copy-start
  6.5 0.0 all-gather.3.cloned.1.call-start
  6.5 0.9 copy.20
  7.4 0.1 eq.29
  7.5 0.1 eq.25
  7.6 0.7 broadcast_multiply_fusion
  8.3 1.2 reduce-window.6
  9.5 0.2 slice_reduce_fusion
  9.8 0.1 copy.19
  9.9 0.1 mul.38
  10.0 27.1 %all_gather.6 = bf16[64,4096]{1,0:T(8,128)(2,1)S(1)} all-gather(bf16[64,512]{1,0:T(8,128)(2,1)} %param.6), channel_id=1, replica_groups=mesh['expert'=64,'hidden'=8] {'hidden'}, dimensions={1}, use_global_device_ids=true | all-gather | bytes 589824 | tf_op jit(solution)/shard_map/all_gather | solution.py:20
  37.1 0.1 fusion.29
  37.3 4.4 %gather_fusion = bf16[512,4096]{1,0:T(8,128)(2,1)} fusion(bf16[64,4096]{1,0:T(8,128)(2,1)S(1)} %all_gather.6, s32[1024]{0:T(1024)S(1)} %pad_clamp_fusion.1), kind=kCustom, calls=%fused_computation | custom fusion | bytes 8390656 | tf_op jit(solution)/shard_map/gather | solution.py:22
  41.6 12.4 %scatter_custom_fusion = bf16[1024,4096]{1,0:T(8,128)(2,1)} fusion(s32[512]{0:T(512)S(1)} %bitcast.75, bf16[512,4096]{1,0:T(8,128)(2,1)} %gather_fusion, bf16[]{:T(256)} %constant.26.clone.1), kind=kCustom, calls=%fused_computation.3 | custom fusion | bytes 8389120 | tf_op jit(solution)/shard_map/scatter | solution.py:22
  54.1 201.0 %all_to_all.8 = bf16[64,16,4096]{2,1,0:T(8,128)(2,1)S(1)} all-to-all(bf16[64,16,4096]{2,1,0:T(8,128)(2,1)} %bitcast.68), channel_id=1, replica_groups=mesh['expert'=64,'hidden'=8] {'expert'}, dimensions={0} | all-to-all | bytes 16777216 | tf_op jit(solution)/shard_map/all_to_all | solution.py:23
  255.0 2.9 fusion.14
  258.0 3.7 fusion.23
  261.7 0.0 all-gather.3.cloned.1.call-update
  261.7 43.4 %all-gather.3.cloned.1.call-done = bf16[1536,1024]{1,0:T(8,128)(2,1)} async-done(((bf16[192,1024]{1,0:T(8,128)(2,1)}), bf16[1536,1024]{1,0:T(8,128)(2,1)}) %all-gather.3.cloned.1.call-update) | async-done | bytes 3145744 | tf_op jit(solution)/shard_map/all_gather | solution.py:35
  305.1 3.7 fusion.11
  308.8 3.0 copy.31
  311.8 0.5 broadcast.125
  312.3 8.3 %reduce.2 = bf16[1024,512]{1,0:T(8,128)(2,1)S(1)} reduce(bf16[1024,1,512]{2,1,0:T(2,128)(2,1)} %bitcast.73, bf16[]{:T(256)} %broadcast.125), dimensions={1}, to_apply=%bitcast.67.reduce_sub_computation | reduce | bytes 2097154
  320.6 1.6 reshape.173
  322.2 10.3 %all-to-all-start.1 = ((bf16[64,2,4096]{2,1,0:T(2,128)(2,1)}), bf16[64,2,4096]{2,1,0:T(2,128)(2,1)S(1)}, u32[]{:S(2)}, u32[]{:S(2)}) async-start(bf16[64,2,4096]{2,1,0:T(2,128)(2,1)} %reshape.173), calls=%async_computation.1 | async-start | bytes 2097152 | tf_op jit(solution)/shard_map/all_to_all | solution.py:39
  332.5 0.0 copy-done.1
  332.5 0.1 copy.24
  332.6 27.9 %all-to-all-done.1 = bf16[64,2,4096]{2,1,0:T(2,128)(2,1)S(1)} async-done(((bf16[64,2,4096]{2,1,0:T(2,128)(2,1)}), bf16[64,2,4096]{2,1,0:T(2,128)(2,1)S(1)}, u32[]{:S(2)}, u32[]{:S(2)}) %all-to-all-start.1) | async-done | bytes 1048608 | tf_op jit(solution)/shard_map/all_to_all | solution.py:39
  360.5 3.5 reshape.174
  364.0 1.9 copy.30
  365.9 2.0 gather_fusion.1
  367.8 1.0 fusion.26
  (13 shorter events, 0.1 us)
Async XLA Ops:
  6.5 298.6 %copy-start = (bf16[1,1536,512]{2,1,0:T(8,128)(2,1)S(1)}, bf16[1,1536,512]{2,1,0:T(8,128)(2,1)}, u32[]{:S(2)}) copy-start(bf16[1,1536,512]{2,1,0:T(8,128)(2,1)} %param.11) | copy-start | bytes 4718596
  6.5 298.6 %all-gather.3.cloned.1.call-start = ((), (), s32[]{:S(2)}) async-start(), calls=%async_computation.2 | async-start | bytes 3538944 | tf_op jit(solution)/shard_map/all_gather | solution.py:35
  54.1 201.0 %copy-start.2 = (bf16[1,192,4096]{2,1,0:T(8,128)(2,1)S(1)}, bf16[1,192,4096]{2,1,0:T(8,128)(2,1)}, u32[]{:S(2)}) copy-start(bf16[1,192,4096]{2,1,0:T(8,128)(2,1)} %param.9) | copy-start | bytes 4718596
  255.0 2.9 copy-start.3
  311.8 20.7 %copy-start.1 = (f32[64,8]{0,1:T(8,128)S(1)}, f32[64,8]{0,1:T(8,128)}, u32[]{:S(2)}) copy-start(f32[64,8]{0,1:T(8,128)} %param.8) | copy-start | bytes 6148
  322.2 38.3 %all-to-all-start.1 = ((bf16[64,2,4096]{2,1,0:T(2,128)(2,1)}), bf16[64,2,4096]{2,1,0:T(2,128)(2,1)S(1)}, u32[]{:S(2)}, u32[]{:S(2)}) async-start(bf16[64,2,4096]{2,1,0:T(2,128)(2,1)} %reshape.173), calls=%async_computation.1 | async-start | bytes 2097152 | tf_op jit(solution)/shard_map/all_to_all | solution.py:39
Sparse Core Ops, SparseCore 0:
  261.8 43.2 all-gather.2
where the time goes:
time: 376 us
  blocking collectives  228 us (61%)
  waiting for transfers between devices  71.3 us (19%)
  local copies, waits for them, and re-layouts  30.8 us (8%)
  between operations  13.5 us (4%)
  other arithmetic  11.3 us (3%)
  starting transfers between devices  10.4 us (3%)
  matrix products  10.3 us (3%)
    all_to_all x1, blocking collectives, on_device(): lax.all_to_all(packed.reshape(experts_all, capacity, full_rows.shape[1]),...  201 us
    all_gather x1, waiting for transfers between devices, on_device(): lax.all_gather(activation, 'hidden', axis=1, tiled=True)  43.4 us
    all_to_all x1, waiting for transfers between devices, on_device(): lax.all_to_all(expert_out, 'expert', split_axis=1, concat_axis=0, tiled=T...  27.9 us
    all_gather x1, blocking collectives, on_device(): full_rows = lax.all_gather(tokens, 'hidden', axis=1, tiled=True)  27.1 us
    scatter x1, local copies, waits for them, and re-layouts, on_device(): packed = packed.at[position].set(full_rows[token_of])  12.4 us
    all_to_all x1, starting transfers between devices, on_device(): lax.all_to_all(expert_out, 'expert', split_axis=1, concat_axis=0, tiled=T...  10.3 us
    unnamed x14, local copies, waits for them, and re-layouts  8.43 us
    unnamed x1, other arithmetic  8.25 us
  transfers between devices with their start and end apart: 2, of which 2 were waited for; matrix products, arithmetic and copies ran while one was open for 0% of the time, Pallas kernels for 0%

commit v1 on v0

--- a/solution.py
+++ b/solution.py
@@ -2,6 +2,27 @@
 import jax.numpy as jnp
 from jax import lax
 from jax.sharding import PartitionSpec as P
+
+
+def gather_around(x, axis, dim):
+    count, mine, rows = (lax.axis_size(axis), lax.axis_index(axis), x.shape[dim])
+    forward = [(i, (i + 1) % count) for i in range(count)]
+    left = [(i, (i - 1) % count) for i in range(count)]
+    filled = jnp.zeros((*x.shape[:dim], count * rows, *x.shape[dim + 1 :]), x.dtype)
+    filled = lax.dynamic_update_slice_in_dim(filled, x, mine * rows, axis=dim)
+    from_left = from_right = x
+    half = count // 2
+    for hop in range(1, half + 1):
+        from_left = lax.ppermute(from_left, axis, forward)
+        filled = lax.dynamic_update_slice_in_dim(
+            filled, from_left, (mine - hop) % count * rows, axis=dim
+        )
+        if hop < count - half:
+            from_right = lax.ppermute(from_right, axis, left)
+            filled = lax.dynamic_update_slice_in_dim(
+                filled, from_right, (mine + hop) % count * rows, axis=dim
+            )
+    return filled
 
 
 def on_device(tokens, expert_ids, gate_weights, gate_proj, up_proj, down_proj):
@@ -32,7 +53,7 @@
     activation = (jax.nn.silu(gate_sum) * up_sum).astype(jnp.bfloat16)
     expert_out = jnp.einsum(
         "lfr,lfd->lrd",
-        lax.all_gather(activation, "hidden", axis=1, tiled=True),
+        gather_around(activation, "hidden", 1),
         down_proj,
         preferred_element_type=jnp.float32,
     ).astype(jnp.bfloat16)

time: 376 us -> 381 us (1.013)
  blocking collectives: 228 us -> 27.1 us
  waiting for transfers between devices: 71.3 us -> 225 us
  starting transfers between devices: 10.4 us -> 60.7 us
  between operations: 13.5 us -> 0.3 us
  local copies, waits for them, and re-layouts: 30.8 us -> 38.5 us
  matrix products: 10.3 us -> 17.5 us
    all_to_all x1 -> x0, blocking collectives: 201 us -> none  [on_device(): lax.all_to_all(packed.reshape(experts_all, capacity, full_rows.shape[1]),...]
    all_to_all x0 -> x1, waiting for transfers between devices: none -> 182 us  [on_device(): lax.all_to_all(packed.reshape(experts_all, capacity, full_rows.shape[1]),...]
    all_gather x1 -> x0, waiting for transfers between devices: 43.4 us -> none  [on_device(): lax.all_gather(activation, 'hidden', axis=1, tiled=True)]
    ppermute x0 -> x7, starting transfers between devices: none -> 21.1 us  [the longest x3 11.7 us: gather_around(): from_right = lax.ppermute(from_right, axis, left)]
    all_to_all x0 -> x1, starting transfers between devices: none -> 16.7 us  [on_device(): lax.all_to_all(packed.reshape(experts_all, capacity, full_rows.shape[1]),...]
    ppermute x0 -> x7, waiting for transfers between devices: none -> 14.5 us  [the longest x4 14.2 us: gather_around(): from_left = lax.ppermute(from_left, axis, forward)]
    all_to_all x1, starting transfers between devices: 10.3 us -> 22.9 us  [on_device(): lax.all_to_all(expert_out, 'expert', split_axis=1, concat_axis=0, tiled=T...]
    dynamic_update_slice x0 -> x7, local copies, waits for them, and re-layouts: none -> 5.56 us  [the longest x4 3.17 us: gather_around(): lax.dynamic_update_slice_in_dim(filled, from_left, (mine - hop) % count *...]
  transfers between devices with their start and end apart: 2 -> 9, of which waited for: 2 -> 7; matrix products, arithmetic and copies ran while one was open for 0% -> 1% of each run, Pallas kernels for 0% -> 0%
where the time goes in v1:
time: 381 us; the launch traced here: 380 us
  waiting for transfers between devices  225 us (59%)
  starting transfers between devices  60.7 us (16%)
  local copies, waits for them, and re-layouts  38.5 us (10%)
  blocking collectives  27.1 us (7%)
  matrix products  17.5 us (5%)
  other arithmetic  11.1 us (3%)
    all_to_all x1, waiting for transfers between devices, on_device(): lax.all_to_all(packed.reshape(experts_all, capacity, full_rows.shape[1]),...  182 us
    all_to_all x1, waiting for transfers between devices, on_device(): lax.all_to_all(expert_out, 'expert', split_axis=1, concat_axis=0, tiled=T...  27.9 us
    all_gather x1, blocking collectives, on_device(): full_rows = lax.all_gather(tokens, 'hidden', axis=1, tiled=True)  27.1 us
    all_to_all x1, starting transfers between devices, on_device(): lax.all_to_all(expert_out, 'expert', split_axis=1, concat_axis=0, tiled=T...  22.9 us
    all_to_all x1, starting transfers between devices, on_device(): lax.all_to_all(packed.reshape(experts_all, capacity, full_rows.shape[1]),...  16.7 us
    ppermute x4, waiting for transfers between devices, gather_around(): from_left = lax.ppermute(from_left, axis, forward)  14.2 us
    scatter x1, local copies, waits for them, and re-layouts, on_device(): packed = packed.at[position].set(full_rows[token_of])  12.4 us
    ppermute x3, starting transfers between devices, gather_around(): from_right = lax.ppermute(from_right, axis, left)  11.7 us
  transfers between devices with their start and end apart: 9, of which 7 were waited for; matrix products, arithmetic and copies ran while one was open for 1% of the time, Pallas kernels for 0%

profile of v1, /device:TPU:1, one launch (start us, length us, event | category | flops | bytes accessed | tf_op | source)
XLA Modules:
  0.0 380.0 jit_solution(16325157703490130457)
XLA Ops:
  0.0 0.9 copy.20
  1.8 1.2 reduce-window.6
  3.5 27.1 %all_gather.3 = bf16[64,4096]{1,0:T(8,128)(2,1)S(1)} all-gather(bf16[64,512]{1,0:T(8,128)(2,1)} %param.6), channel_id=1, replica_groups=mesh['expert'=64,'hidden'=8] {'hidden'}, dimensions={1}, use_global_device_ids=true | all-gather | bytes 589824 | tf_op jit(solution)/shard_map/all_gather | solution.py:41
  30.7 4.4 %gather_fusion = bf16[512,4096]{1,0:T(8,128)(2,1)} fusion(bf16[64,4096]{1,0:T(8,128)(2,1)S(1)} %all_gather.3, s32[1024]{0:T(1024)S(1)} %pad_clamp_fusion.1), kind=kCustom, calls=%fused_computation | custom fusion | bytes 8390656 | tf_op jit(solution)/shard_map/gather | solution.py:43
  35.1 12.4 %scatter_custom_fusion = bf16[1024,4096]{1,0:T(8,128)(2,1)} fusion(s32[512]{0:T(512)S(1)} %bitcast.90, bf16[512,4096]{1,0:T(8,128)(2,1)} %gather_fusion, bf16[]{:T(256)} %constant.81.clone.1), kind=kCustom, calls=%fused_computation.3 | custom fusion | bytes 8389120 | tf_op jit(solution)/shard_map/scatter | solution.py:43
  47.5 16.7 %all-to-all-start = ((bf16[64,16,4096]{2,1,0:T(8,128)(2,1)}), bf16[64,16,4096]{2,1,0:T(8,128)(2,1)}, u32[]{:S(2)}, u32[]{:S(2)}) async-start(bf16[64,16,4096]{2,1,0:T(8,128)(2,1)} %bitcast.85), calls=%async_computation | async-start | bytes 16777216 | tf_op jit(solution)/shard_map/all_to_all | solution.py:44
  64.2 182.4 %all-to-all-done = bf16[64,16,4096]{2,1,0:T(8,128)(2,1)} async-done(((bf16[64,16,4096]{2,1,0:T(8,128)(2,1)}), bf16[64,16,4096]{2,1,0:T(8,128)(2,1)}, u32[]{:S(2)}, u32[]{:S(2)}) %all-to-all-start) | async-done | bytes 8388640 | tf_op jit(solution)/shard_map/all_to_all | solution.py:44
  246.6 6.7 %fusion.14 = f32[192,1024]{1,0:T(8,128)S(1)} fusion(bf16[1024,4096]{1,0:T(8,128)(2,1)} %bitcast.5, bf16[1,192,4096]{2,1,0:T(8,128)(2,1)} %param.9), kind=kOutput, calls=%fused_computation.13 | convolution fusion | flops 1610612736 | bytes 10747904 | tf_op jit(solution)/shard_map/lrd,lfd->lfr/dot_general | solution.py:51
  253.3 2.2 broadcast.119
  255.5 7.1 %constant_dynamic-update-slice_fusion = (bf16[1536,1024]{1,0:T(8,128)(2,1)}, bf16[192,1024]{1,0:T(8,128)(2,1)S(1)}) fusion(bf16[1536,1024]{1,0:T(8,128)(2,1)} %broadcast.119, s32[]{:T(128)S(6)} %select_n.91, bf16[1024,4096]{1,0:T(8,128)(2,1)} %bitcast.5, bf16[1,192,4096]{2,1,0:T(8,128)(2,1)S(1)} %copy-done, f32[192,1024]{1,0:T(8,128)S(1)} %fusion.14), kind=kOutput, calls=%fused_computation.44 | convolution fusion | flops 1611792384 | bytes 11534340 | tf_op jit(solution)/shard_map/lrd,lfd->lfr/dot_general | solution.py:52
  262.6 3.4 collective-permute-start
  266.0 3.1 collective-permute-start.1
  269.2 3.1 collective-permute-done
  272.3 2.2 collective-permute-start.2
  274.8 4.0 %collective-permute-start.3 = (bf16[1,192,1024]{2,1,0:T(8,128)(2,1)S(1)}, bf16[1,192,1024]{2,1,0:T(8,128)(2,1)S(1)}, u32[]{:S(2)}, u32[]{:S(2)}) collective-permute-start(bf16[1,192,1024]{2,1,0:T(8,128)(2,1)S(1)} %collective-permute-done.1), channel_id=1, source_target_pairs={{0,7},{1,0},{2,1},{3,2},{4,3},{5,4},{6,5},{7,6},{8,15},{9,8},{10,9... | collective-permute-start | bytes 1179656 | tf_op jit(solution)/shard_map/ppermute | solution.py:21
  279.6 0.8 bitcast_dynamic-update-slice_fusion.5
  280.4 1.6 collective-permute-done.2
  282.0 1.9 collective-permute-start.4
  284.0 4.6 %collective-permute-start.5 = (bf16[1,192,1024]{2,1,0:T(8,128)(2,1)S(1)}, bf16[1,192,1024]{2,1,0:T(8,128)(2,1)S(1)}, u32[]{:S(2)}, u32[]{:S(2)}) collective-permute-start(bf16[1,192,1024]{2,1,0:T(8,128)(2,1)S(1)} %collective-permute-done.3), channel_id=1, source_target_pairs={{0,7},{1,0},{2,1},{3,2},{4,3},{5,4},{6,5},{7,6},{8,15},{9,8},{10,9... | collective-permute-start | bytes 1179656 | tf_op jit(solution)/shard_map/ppermute | solution.py:21
  290.2 1.9 collective-permute-done.4
  292.1 1.9 collective-permute-start.6
  295.6 7.6 %collective-permute-done.6 = bf16[1,192,1024]{2,1,0:T(8,128)(2,1)S(1)} collective-permute-done((bf16[1,192,1024]{2,1,0:T(8,128)(2,1)S(1)}, bf16[1,192,1024]{2,1,0:T(8,128)(2,1)S(1)}, u32[]{:S(2)}, u32[]{:S(2)}) %collective-permute-start.6) | collective-permute-done | bytes 393248 | tf_op jit(solution)/shard_map/ppermute | solution.py:16
  303.9 3.7 fusion.11
  307.7 3.0 copy.31
  311.2 8.0 %reduce.2 = bf16[1024,512]{1,0:T(8,128)(2,1)S(1)} reduce(bf16[1024,1,512]{2,1,0:T(2,128)(2,1)} %bitcast.88, bf16[]{:T(256)} %broadcast.141), dimensions={1}, to_apply=%bitcast.84.reduce_sub_computation | reduce | bytes 2097154
  319.2 1.6 reshape.206
  320.8 22.9 %all-to-all-start.1 = ((bf16[64,2,4096]{2,1,0:T(2,128)(2,1)}), bf16[64,2,4096]{2,1,0:T(2,128)(2,1)S(1)}, u32[]{:S(2)}, u32[]{:S(2)}) async-start(bf16[64,2,4096]{2,1,0:T(2,128)(2,1)} %reshape.206), calls=%async_computation.1 | async-start | bytes 2097152 | tf_op jit(solution)/shard_map/all_to_all | solution.py:60
  343.8 27.9 %all-to-all-done.1 = bf16[64,2,4096]{2,1,0:T(2,128)(2,1)S(1)} async-done(((bf16[64,2,4096]{2,1,0:T(2,128)(2,1)}), bf16[64,2,4096]{2,1,0:T(2,128)(2,1)S(1)}, u32[]{:S(2)}, u32[]{:S(2)}) %all-to-all-start.1) | async-done | bytes 1048608 | tf_op jit(solution)/shard_map/all_to_all | solution.py:60
  371.7 3.5 reshape.207
  375.2 1.9 copy.30
  377.1 2.0 gather_fusion.1
  379.0 1.0 fusion.26
  (31 shorter events, 7.2 us)
Async XLA Ops:
  0.0 255.5 %copy-start = (bf16[1,192,4096]{2,1,0:T(8,128)(2,1)S(1)}, bf16[1,192,4096]{2,1,0:T(8,128)(2,1)}, u32[]{:S(2)}) copy-start(bf16[1,192,4096]{2,1,0:T(8,128)(2,1)} %param.10) | copy-start | bytes 4718596
  47.5 199.1 %all-to-all-start = ((bf16[64,16,4096]{2,1,0:T(8,128)(2,1)}), bf16[64,16,4096]{2,1,0:T(8,128)(2,1)}, u32[]{:S(2)}, u32[]{:S(2)}) async-start(bf16[64,16,4096]{2,1,0:T(8,128)(2,1)} %bitcast.85), calls=%async_computation | async-start | bytes 16777216 | tf_op jit(solution)/shard_map/all_to_all | solution.py:44
  262.6 9.7 %collective-permute-start = (bf16[1,192,1024]{2,1,0:T(8,128)(2,1)S(1)}, bf16[1,192,1024]{2,1,0:T(8,128)(2,1)S(1)}, u32[]{:S(2)}, u32[]{:S(2)}) collective-permute-start(bf16[1,192,1024]{2,1,0:T(8,128)(2,1)S(1)} %bitcast.93), channel_id=1, source_target_pairs={{0,1},{1,2},{2,3},{3,4},{4,5},{5,6},{6,7},{7,0},{8,9},{9,10},{10,1... | collective-permute-start | bytes 1179656 | tf_op jit(solution)/shard_map/ppermute | solution.py:16
  266.0 8.8 %collective-permute-start.1 = (bf16[1,192,1024]{2,1,0:T(8,128)(2,1)S(1)}, bf16[1,192,1024]{2,1,0:T(8,128)(2,1)S(1)}, u32[]{:S(2)}, u32[]{:S(2)}) collective-permute-start(bf16[1,192,1024]{2,1,0:T(8,128)(2,1)S(1)} %bitcast.94), channel_id=1, source_target_pairs={{0,7},{1,0},{2,1},{3,2},{4,3},{5,4},{6,5},{7,6},{8,15},{9,8},{10,9... | collective-permute-start | bytes 1179656 | tf_op jit(solution)/shard_map/ppermute | solution.py:21
  269.2 34.7 %copy-start.2 = (bf16[1,1536,512]{2,1,0:T(8,128)(2,1)S(1)}, bf16[1,1536,512]{2,1,0:T(8,128)(2,1)}, u32[]{:S(2)}) copy-start(bf16[1,1536,512]{2,1,0:T(8,128)(2,1)} %param.11) | copy-start | bytes 4718596
  272.3 9.7 %collective-permute-start.2 = (bf16[1,192,1024]{2,1,0:T(8,128)(2,1)S(1)}, bf16[1,192,1024]{2,1,0:T(8,128)(2,1)S(1)}, u32[]{:S(2)}, u32[]{:S(2)}) collective-permute-start(bf16[1,192,1024]{2,1,0:T(8,128)(2,1)S(1)} %collective-permute-done), channel_id=1, source_target_pairs={{0,1},{1,2},{2,3},{3,4},{4,5},{5,6},{6,7},{7,0},{8,9},{9,10},{10,1... | collective-permute-start | bytes 1179656 | tf_op jit(solution)/shard_map/ppermute | solution.py:16
  274.8 9.2 %collective-permute-start.3 = (bf16[1,192,1024]{2,1,0:T(8,128)(2,1)S(1)}, bf16[1,192,1024]{2,1,0:T(8,128)(2,1)S(1)}, u32[]{:S(2)}, u32[]{:S(2)}) collective-permute-start(bf16[1,192,1024]{2,1,0:T(8,128)(2,1)S(1)} %collective-permute-done.1), channel_id=1, source_target_pairs={{0,7},{1,0},{2,1},{3,2},{4,3},{5,4},{6,5},{7,6},{8,15},{9,8},{10,9... | collective-permute-start | bytes 1179656 | tf_op jit(solution)/shard_map/ppermute | solution.py:21
  282.0 10.0 %collective-permute-start.4 = (bf16[1,192,1024]{2,1,0:T(8,128)(2,1)S(1)}, bf16[1,192,1024]{2,1,0:T(8,128)(2,1)S(1)}, u32[]{:S(2)}, u32[]{:S(2)}) collective-permute-start(bf16[1,192,1024]{2,1,0:T(8,128)(2,1)S(1)} %collective-permute-done.2), channel_id=1, source_target_pairs={{0,1},{1,2},{2,3},{3,4},{4,5},{5,6},{6,7},{7,0},{8,9},{9,10},{10,1... | collective-permute-start | bytes 1179656 | tf_op jit(solution)/shard_map/ppermute | solution.py:16
  284.0 10.8 %collective-permute-start.5 = (bf16[1,192,1024]{2,1,0:T(8,128)(2,1)S(1)}, bf16[1,192,1024]{2,1,0:T(8,128)(2,1)S(1)}, u32[]{:S(2)}, u32[]{:S(2)}) collective-permute-start(bf16[1,192,1024]{2,1,0:T(8,128)(2,1)S(1)} %collective-permute-done.3), channel_id=1, source_target_pairs={{0,7},{1,0},{2,1},{3,2},{4,3},{5,4},{6,5},{7,6},{8,15},{9,8},{10,9... | collective-permute-start | bytes 1179656 | tf_op jit(solution)/shard_map/ppermute | solution.py:21
  292.1 11.1 %collective-permute-start.6 = (bf16[1,192,1024]{2,1,0:T(8,128)(2,1)S(1)}, bf16[1,192,1024]{2,1,0:T(8,128)(2,1)S(1)}, u32[]{:S(2)}, u32[]{:S(2)}) collective-permute-start(bf16[1,192,1024]{2,1,0:T(8,128)(2,1)S(1)} %collective-permute-done.4), channel_id=1, source_target_pairs={{0,1},{1,2},{2,3},{3,4},{4,5},{5,6},{6,7},{7,0},{8,9},{9,10},{10,1... | collective-permute-start | bytes 1179656 | tf_op jit(solution)/shard_map/ppermute | solution.py:16
  311.2 32.6 %copy-start.1 = (f32[64,8]{0,1:T(8,128)S(1)}, f32[64,8]{0,1:T(8,128)}, u32[]{:S(2)}) copy-start(f32[64,8]{0,1:T(8,128)} %param.8) | copy-start | bytes 6148
  320.8 50.9 %all-to-all-start.1 = ((bf16[64,2,4096]{2,1,0:T(2,128)(2,1)}), bf16[64,2,4096]{2,1,0:T(2,128)(2,1)S(1)}, u32[]{:S(2)}, u32[]{:S(2)}) async-start(bf16[64,2,4096]{2,1,0:T(2,128)(2,1)} %reshape.206), calls=%async_computation.1 | async-start | bytes 2097152 | tf_op jit(solution)/shard_map/all_to_all | solution.py:60
